TPU v7x, 128 devices: a whole 4x4x4 slice. The times are simulated.
128 devices in a mesh: row: 8 (over y, core), col: 16 (over z, x).
Axes of the slice: x: 4, y: 4, z: 4, core: 2. Of those that a mesh axis runs over, the one named last changes fastest.
Arguments:
- ancestor_inverse: float32 [12288, 12288], P('row', 'col')
- factor: bfloat16 [3, 12288, 512], P(None, ('row', 'col')), may hold values from -0.5 to 0.5
- coupling: float32 [3, 512, 512], replicated, may hold values from -0.25 to 0.25
- diagonal_inverse: float32 [3, 512, 512], replicated, may hold values from -6 to 6
- ancestors: int32 [3, 24], replicated, may hold values from -1 to 23, as said below
Outputs:
- block_columns: float32 [3, 12288, 512], P(None, ('row', 'col'))
- block_rows: float32 [3, 12288, 512], P(None, ('col', 'row'))
- node_blocks: float32 [3, 3, 512, 512], replicated
Inputs may be any that keep to these rules, and one draw needn't show every extreme that they name: `ancestors`: row k lists the ancestor block rows of supernode k, blocks of 512 rows: distinct indices in increasing order, then -1 in the slots left. Every block is listed by some supernode.
All inputs are finite; a program needn't handle non-finite values.
Results may differ from a plain program's by a relative error of at most 0.0003.
Values may be sent and summed in bfloat16 or wider, within the bound.
A program may use at most 128 MiB of HBM per device.

v0:
```python
import jax
import jax.numpy as jnp
from jax import lax
from jax.sharding import PartitionSpec as P

highest = lax.Precision.HIGHEST


def broadcast(value, axis, source):
    kept = jnp.where(lax.axis_index(axis) == source, value, 0).astype(value.dtype)
    return lax.psum(kept, axis)


def matmul(left, right):
    return jnp.dot(left, right, precision=highest)


def left_dot(left, right):
    return lax.dot_general(left, right, (((0,), (0,)), ((), ())), precision=highest)


def pair_index(later, earlier):
    return later * (later - 1) // 2 + earlier


def local(ancestor_inverse, factor, coupling, diagonal_inverse, ancestors):
    col_count = lax.axis_size("col")
    row_count = lax.axis_size("row")
    row_index = lax.axis_index("row")
    col_index = lax.axis_index("col")
    nodes_total, piece_rows, sn_width = factor.shape
    rows_here, cols_here = ancestor_inverse.shape
    group_ratio = rows_here // cols_here
    first_row = (row_index * col_count + col_index) * piece_rows
    block_of_row = (first_row + jnp.arange(piece_rows, dtype=jnp.int32)) // sn_width
    source_row = col_index // group_ratio
    block_start = col_index % group_ratio * cols_here
    row_layout = []
    solved = {}
    for current in range(nodes_total):
        listed = jnp.any(ancestors[current][:, None] == block_of_row[None, :], axis=0)
        lower_part = jnp.where(listed[:, None], factor[current], jnp.zeros_like(factor[current]))
        lower_rows = lax.all_gather(lower_part, "col", axis=0, tiled=True)
        own_block = lax.dynamic_slice_in_dim(lower_rows, block_start, cols_here, 0)
        lower_cols = broadcast(own_block, "row", source_row).astype(jnp.float32)
        lower_here = lower_part.astype(jnp.float32)
        product_sum = lax.psum_scatter(
            matmul(ancestor_inverse, lower_cols), "col", scatter_dimension=0, tiled=True
        )
        for earlier in range(current):
            product_sum = product_sum + matmul(
                row_layout[earlier], coupling[pair_index(current, earlier)]
            )
        column = -product_sum
        stacked = jnp.concatenate(row_layout + [column], axis=1)
        summed = lax.psum(left_dot(lower_here, stacked), ("row", "col"))
        crosses = [
            summed[:, earlier * sn_width : (earlier + 1) * sn_width] for earlier in range(current)
        ]
        self_term = summed[:, current * sn_width : (current + 1) * sn_width]
        for earlier in range(current):
            block_value = -crosses[earlier].T
            for inner in range(current):
                block_value = block_value - matmul(
                    solved[earlier, inner], coupling[pair_index(current, inner)]
                )
            solved[earlier, current] = block_value
            solved[current, earlier] = block_value.T
        diag_value = diagonal_inverse[current] - self_term
        for earlier in range(current):
            diag_value = diag_value - left_dot(
                coupling[pair_index(current, earlier)], solved[earlier, current]
            )
        solved[current, current] = diag_value
        row_layout.append(column)
    finished = jnp.stack(row_layout)
    part_rows = piece_rows // row_count
    ratio_cols = col_count // row_count
    split_parts = finished.reshape(nodes_total, row_count, part_rows, sn_width)
    held = lax.all_to_all(split_parts, "row", split_axis=1, concat_axis=1, tiled=True)
    targets = jnp.arange(row_count, dtype=jnp.int32) * ratio_cols + col_index // row_count
    onehot = (targets[:, None] == jnp.arange(col_count, dtype=jnp.int32)[None, :]).astype(
        jnp.float32
    )
    slotted = jnp.einsum("rc,nrqs->ncqs", onehot, held, precision=highest)
    arrived = lax.all_to_all(slotted, "col", split_axis=1, concat_axis=1, tiled=True)
    picked = lax.dynamic_slice_in_dim(arrived, col_index % ratio_cols * row_count, row_count, 1)
    landed = lax.all_to_all(picked, "row", split_axis=1, concat_axis=1, tiled=True)
    mirrored_all = landed.reshape(nodes_total, piece_rows, sn_width)
    node_blocks = jnp.stack(
        [
            jnp.stack([solved[first_node, second_node] for second_node in range(nodes_total)])
            for first_node in range(nodes_total)
        ]
    )
    return (finished, mirrored_all, node_blocks)


def solution(mesh):
    placed = (P("row", "col"), P(None, ("row", "col"), None), P(), P(), P())
    return jax.shard_map(
        local,
        mesh=mesh,
        in_specs=placed,
        out_specs=(P(None, ("row", "col"), None), P(None, ("col", "row"), None), P()),
        check_vma=False,
    )
```

profile of v0, /device:TPU:1, one launch (start us, length us, event | category | flops | bytes accessed | tf_op | source)
XLA Modules:
  0.0 691.0 jit_solution(10552824575240240170)
XLA Ops:
  7.2 0.8 slice_bitcast_fusion.2
  8.1 1.8 bitcast_select_fusion.1
  10.0 0.7 all-gather.4.cloned.1.call-update
  11.5 45.6 %all-gather.6.cloned.1.call-done = bf16[1536,512]{1,0:T(8,128)(2,1)} async-done(((bf16[96,512]{1,0:T(8,128)(2,1)}), bf16[1536,512]{1,0:T(8,128)(2,1)}) %all-gather.6.cloned.1.call-update) | async-done | bytes 1572880 | tf_op jit(solution)/shard_map/all_gather | solution.py:43
  57.1 2.2 dynamic-slice_select_fusion.1
  59.2 43.3 %all-gather.4.cloned.1.call-done = bf16[1536,512]{1,0:T(8,128)(2,1)} async-done(((bf16[96,512]{1,0:T(8,128)(2,1)}), bf16[1536,512]{1,0:T(8,128)(2,1)}) %all-gather.4.cloned.1.call-update) | async-done | bytes 1572880 | tf_op jit(solution)/shard_map/all_gather | solution.py:43
  102.5 2.1 dynamic-slice_select_fusion.2
  104.7 43.3 %all-gather.8.cloned.1.call-done = bf16[1536,512]{1,0:T(8,128)(2,1)} async-done(((bf16[96,512]{1,0:T(8,128)(2,1)}), bf16[1536,512]{1,0:T(8,128)(2,1)}) %all-gather.8.cloned.1.call-update) | async-done | bytes 1572880 | tf_op jit(solution)/shard_map/all_gather | solution.py:43
  148.0 2.1 dynamic-slice_select_fusion
  150.3 66.0 %all-reduce.7.cloned.1.call-done = (bf16[768,512]{1,0:T(8,128)(2,1)}, bf16[768,512]{1,0:T(8,128)(2,1)}, bf16[768,512]{1,0:T(8,128)(2,1)}) async-done(((bf16[768,512]{1,0:T(8,128)(2,1)}, bf16[768,512]{1,0:T(8,128)(2,1)}, bf16[768,512]{1,0:T(8,128)(2,1)}), (bf16[768,512]{1,0:T(8,128)(2,1)}, bf16[768,512]{1,0:T(8,128)(2,1)}, bf16[768,512]{1,0:T(8,128)(2,1)})) %all-reduce.7.cloned.1.call-update) | async-done | bytes 2359312 | tf_op jit(solution)/shard_map/psum | solution.py:11
  216.2 6.7 convolution_bitcast_fusion.2
  222.9 2.3 copy.104
  225.3 6.7 convolution_bitcast_fusion.1
  232.0 2.4 copy.106
  234.5 6.7 convolution_bitcast_fusion
  241.2 2.4 copy.108
  244.1 57.1 %reduce-scatter.10.cloned.1.call-done = f32[96,512]{1,0:T(8,128)} async-done(((f32[1536,512]{1,0:T(8,128)}), f32[96,512]{1,0:T(8,128)}) %reduce-scatter.10.cloned.1.call-update) | async-done | bytes 196624 | tf_op jit(solution)/shard_map/reduce_scatter | solution.py:47
  301.2 78.3 %reduce-scatter.12.cloned.1.call-done = f32[96,512]{1,0:T(8,128)} async-done(((f32[1536,512]{1,0:T(8,128)}), f32[96,512]{1,0:T(8,128)}) %reduce-scatter.12.cloned.1.call-update) | async-done | bytes 196624 | tf_op jit(solution)/shard_map/reduce_scatter | solution.py:47
  379.5 1.8 fusion.5
  381.3 77.3 %reduce-scatter.14.cloned.1.call-done = f32[96,512]{1,0:T(8,128)} async-done(((f32[1536,512]{1,0:T(8,128)}), f32[96,512]{1,0:T(8,128)}) %reduce-scatter.14.cloned.1.call-update) | async-done | bytes 196624 | tf_op jit(solution)/shard_map/reduce_scatter | solution.py:47
  458.6 1.8 convolution_add_fusion.1
  460.4 0.7 fusion.4
  461.2 0.7 fusion.63
  461.9 2.3 fusion.45
  464.2 3.1 fusion.38
  467.4 1.6 fusion.54
  469.0 0.9 copy-done.18
  469.9 0.7 stack.74
  470.6 0.7 stack.73
  471.4 1.6 stack.72
  473.0 1.2 pad_maximum_fusion.1
  474.2 1.0 copy.78
  475.2 6.7 all-to-all-start
  481.9 15.6 %all-to-all-done = f32[3,8,12,512]{3,2,0,1:T(8,128)} async-done(((f32[3,8,12,512]{3,2,0,1:T(8,128)}), f32[3,8,12,512]{3,2,0,1:T(8,128)}, u32[]{:S(2)}, u32[]{:S(2)}) %all-to-all-start) | async-done | bytes 589856 | tf_op jit(solution)/shard_map/all_to_all | solution.py:80
  497.5 2.1 convolution_bitcast_fusion.3
  499.6 1.9 copy.80
  501.5 4.8 all-to-all-start.1
  506.3 21.0 %all-to-all-done.1 = f32[3,16,12,512]{3,2,0,1:T(8,128)} async-done(((f32[3,16,12,512]{3,2,0,1:T(8,128)}), f32[3,16,12,512]{3,2,0,1:T(8,128)}, u32[]{:S(2)}, u32[]{:S(2)}) %all-to-all-start.1) | async-done | bytes 1179680 | tf_op jit(solution)/shard_map/all_to_all | solution.py:86
  527.3 2.1 constant_dynamic-slice_fusion
  529.4 9.0 %all-to-all-start.2 = ((f32[3,8,12,512]{3,2,0,1:T(8,128)}), f32[3,8,12,512]{3,2,0,1:T(8,128)}, u32[]{:S(2)}, u32[]{:S(2)}) async-start(f32[3,8,12,512]{3,2,0,1:T(8,128)} %constant_dynamic-slice_fusion), calls=%async_computation.2 | async-start | bytes 1572864 | tf_op jit(solution)/shard_map/all_to_all | solution.py:88
  538.4 2.4 slice.71
  540.8 2.6 copy.110
  543.4 1.8 pad_maximum_fusion.2
  545.1 5.7 all-to-all-done.2
  550.9 2.2 copy.81
  553.0 2.0 reshape.46
  555.1 83.9 %all-reduce.5.cloned.1.call-done = (f32[512,1536]{1,0:T(8,128)}, f32[512,512]{1,0:T(8,128)}, f32[512,1024]{0,1:T(8,128)}) async-done(((f32[512,1536]{1,0:T(8,128)}, f32[512,512]{1,0:T(8,128)}, f32[512,1024]{0,1:T(8,128)}), (f32[512,1536]{1,0:T(8,128)}, f32[512,512]{1,0:T(8,128)}, f32[512,1024]{0,1:T(8,128)})) %all-reduce.5.cloned.1.call-update) | async-done | bytes 6291472 | tf_op jit(solution)/shard_map/psum | solution.py:56
  638.9 3.8 bitcast_subtract_fusion.7
  642.7 1.9 fusion.14
  644.6 1.9 fusion.18
  646.6 1.9 fusion.20
  648.5 2.0 fusion.3
  650.5 1.0 copy-done.7
  651.5 2.1 fusion.12
  653.7 3.1 fusion.2
  656.8 2.3 fusion.7
  659.1 2.3 fusion.60
  661.4 2.6 copy.85
  663.9 3.8 maximum_bitcast_fusion.1
  667.8 3.6 copy.95
  671.3 4.3 fusion.1
  676.0 0.9 copy-done.13
  677.5 1.6 copy-done.5
  679.1 4.9 pad_maximum_fusion
  (62 shorter events, 2.7 us)
Async XLA Ops:
  7.2 49.9 %all-gather.6.cloned.1.call-start = ((), (), s32[]{:S(2)}) async-start(), calls=%async_computation.7 | async-start | bytes 1671168 | tf_op jit(solution)/shard_map/all_gather | solution.py:43
  9.9 92.6 %all-gather.4.cloned.1.call-start = ((), (), s32[]{:S(2)}) async-start(), calls=%async_computation.6 | async-start | bytes 1671168 | tf_op jit(solution)/shard_map/all_gather | solution.py:43
  10.7 137.4 %all-gather.8.cloned.1.call-start = ((), (), s32[]{:S(2)}) async-start(), calls=%async_computation.8 | async-start | bytes 1671168 | tf_op jit(solution)/shard_map/all_gather | solution.py:43
  11.4 204.8 %all-reduce.7.cloned.1.call-start = ((), (), s32[]{:S(2)}) async-start(), calls=%async_computation.13 | async-start | bytes 4718592 | tf_op jit(solution)/shard_map/psum | solution.py:11
  150.2 151.0 %reduce-scatter.10.cloned.1.call-start = ((), (), s32[]{:S(2)}) async-start(), calls=%async_computation.9 | async-start | bytes 3342336 | tf_op jit(solution)/shard_map/reduce_scatter | solution.py:47
  225.3 154.3 %reduce-scatter.12.cloned.1.call-start = ((), (), s32[]{:S(2)}) async-start(), calls=%async_computation.10 | async-start | bytes 3342336 | tf_op jit(solution)/shard_map/reduce_scatter | solution.py:47
  234.4 224.1 %reduce-scatter.14.cloned.1.call-start = ((), (), s32[]{:S(2)}) async-start(), calls=%async_computation.11 | async-start | bytes 3342336 | tf_op jit(solution)/shard_map/reduce_scatter | solution.py:47
  243.6 136.0 %copy-start = (f32[3,512,512]{2,1,0:T(8,128)S(1)}, f32[3,512,512]{2,1,0:T(8,128)}, u32[]{:S(2)}) copy-start(f32[3,512,512]{2,1,0:T(8,128)} %param.7) | copy-start | bytes 9437188
  243.6 395.3 %all-reduce.5.cloned.1.call-start = ((), (), s32[]{:S(2)}) async-start(), calls=%async_computation.12 | async-start | bytes 12582912 | tf_op jit(solution)/shard_map/psum | solution.py:56
  301.2 159.9 %copy-start.16 = (f32[96,512]{1,0:T(8,128)S(1)}, f32[96,512]{1,0:T(8,128)}, u32[]{:S(2)}) copy-start(f32[96,512]{1,0:T(8,128)} %reduce-scatter.10.cloned.1.call-done) | copy-start | bytes 589828
  458.6 3.3 copy-start.20
  458.6 5.7 copy-start.22
  461.1 6.2 copy-start.17
  461.9 5.5 copy-start.19
  461.9 5.5 copy-start.21
  469.0 0.9 copy-start.18
  475.2 22.3 %all-to-all-start = ((f32[3,8,12,512]{3,2,0,1:T(8,128)}), f32[3,8,12,512]{3,2,0,1:T(8,128)}, u32[]{:S(2)}, u32[]{:S(2)}) async-start(f32[3,8,12,512]{3,2,0,1:T(8,128)} %copy.78), calls=%async_computation | async-start | bytes 1572864 | tf_op jit(solution)/shard_map/all_to_all | solution.py:80
  501.5 25.8 %all-to-all-start.1 = ((f32[3,16,12,512]{3,2,0,1:T(8,128)}), f32[3,16,12,512]{3,2,0,1:T(8,128)}, u32[]{:S(2)}, u32[]{:S(2)}) async-start(f32[3,16,12,512]{3,2,0,1:T(8,128)} %copy.80), calls=%async_computation.1 | async-start | bytes 3145728 | tf_op jit(solution)/shard_map/all_to_all | solution.py:86
  529.4 21.4 %all-to-all-start.2 = ((f32[3,8,12,512]{3,2,0,1:T(8,128)}), f32[3,8,12,512]{3,2,0,1:T(8,128)}, u32[]{:S(2)}, u32[]{:S(2)}) async-start(f32[3,8,12,512]{3,2,0,1:T(8,128)} %constant_dynamic-slice_fusion), calls=%async_computation.2 | async-start | bytes 1572864 | tf_op jit(solution)/shard_map/all_to_all | solution.py:88
  642.7 5.8 copy-start.1
  642.7 3.8 copy-start.8
  642.7 3.8 copy-start.9
  644.6 3.9 copy-start.10
  644.6 3.9 copy-start.11
  646.6 12.5 %copy-start.3 = (f32[512,512]{0,1:T(8,128)}, f32[512,512]{0,1:T(8,128)S(1)}, u32[]{:S(2)}) copy-start(f32[512,512]{0,1:T(8,128)S(1)} %fusion.18) | copy-start | bytes 3145732
  648.5 5.1 copy-start.6
  650.5 1.0 copy-start.7
  653.7 5.4 copy-start.4
  671.3 4.3 copy-start.2
  671.3 4.3 copy-start.12
  671.3 4.3 copy-start.15
  675.7 1.2 copy-start.13
  675.7 1.5 copy-start.14
  677.2 1.9 copy-start.5
Sparse Core Ops, SparseCore 0:
  10.7 46.3 all-gather.5
  59.2 43.3 all-gather.3
  104.7 43.3 all-gather.7
  151.0 65.1 all-reduce.6
  225.4 75.7 reduce-scatter.9
  304.4 75.1 reduce-scatter.11
  383.4 75.0 reduce-scatter.13
  469.1 169.7 all-reduce.4
where the time goes:
time: 699 us; the launch traced here: 691 us
  waiting for transfers between devices  539 us (77%)
  matrix products  54.5 us (8%)
  local copies, waits for them, and re-layouts  36 us (5%)
  other arithmetic  26 us (4%)
  starting transfers between devices  21.2 us (3%)
  between operations  14.7 us (2%)
    reduce_scatter x3, waiting for transfers between devices, local(): lax.psum_scatter(matmul(ancestor_inverse, lower_cols), 'col', scatter_dim...  213 us
    all_gather x3, waiting for transfers between devices, local(): lower_rows = lax.all_gather(lower_part, 'col', axis=0, tiled=True)  132 us
    psum x1, waiting for transfers between devices, local(): summed = lax.psum(left_dot(lower_here, stacked), ('row', 'col'))  83.9 us
    psum x1, waiting for transfers between devices, broadcast(): return lax.psum(kept, axis)  66 us
    dot_general x11, matrix products, matmul(): return jnp.dot(left, right, precision=highest)  36 us
    all_to_all x1, waiting for transfers between devices, local(): lax.all_to_all(slotted, 'col', split_axis=1, concat_axis=1, tiled=True)  21 us
    dot_general x6, matrix products, left_dot(): lax.dot_general(left, right, (((0,), (0,)), ((), ())), precision=highest)  16.5 us
    all_to_all x1, waiting for transfers between devices, local(): lax.all_to_all(split_parts, 'row', split_axis=1, concat_axis=1, tiled=True)  15.6 us
  transfers between devices with their start and end apart: 11, of which 11 were waited for; matrix products, arithmetic and copies ran while one was open for 7% of the time, Pallas kernels for 0%

commit v1 on v0

--- a/solution.py
+++ b/solution.py
@@ -4,6 +4,19 @@
 from jax.sharding import PartitionSpec as P
 
 highest = lax.Precision.HIGHEST
+
+
+def collect(x, axis, dim):
+    ways = lax.axis_size(axis)
+    up = [(d, (d + 1) % ways) for d in range(ways)]
+    down = [(d, (d - 1) % ways) for d in range(ways)]
+    earlier, later = ([x], [x])
+    for _ in range(ways // 2):
+        earlier.append(lax.ppermute(earlier[-1], axis, up))
+    for _ in range((ways - 1) // 2):
+        later.append(lax.ppermute(later[-1], axis, down))
+    line = jnp.concatenate([*earlier[::-1], *later[1:]], axis=dim)
+    return jnp.roll(line, (lax.axis_index(axis) - ways // 2) * x.shape[dim], axis=dim)
 
 
 def broadcast(value, axis, source):
@@ -40,7 +53,7 @@
     for current in range(nodes_total):
         listed = jnp.any(ancestors[current][:, None] == block_of_row[None, :], axis=0)
         lower_part = jnp.where(listed[:, None], factor[current], jnp.zeros_like(factor[current]))
-        lower_rows = lax.all_gather(lower_part, "col", axis=0, tiled=True)
+        lower_rows = collect(lower_part, "col", 0)
         own_block = lax.dynamic_slice_in_dim(lower_rows, block_start, cols_here, 0)
         lower_cols = broadcast(own_block, "row", source_row).astype(jnp.float32)
         lower_here = lower_part.astype(jnp.float32)

time: 699 us -> 675 us (0.966)
  waiting for transfers between devices: 539 us -> 417 us
  starting transfers between devices: 21.2 us -> 109 us
    all_gather x3 -> x0, waiting for transfers between devices: 132 us -> none  [local(): lower_rows = lax.all_gather(lower_part, 'col', axis=0, tiled=True)]
    ppermute x0 -> x45, starting transfers between devices: none -> 88.1 us  [the longest x21 83.7 us: collect(): later.append(lax.ppermute(later[-1], axis, down))]
    psum x1, waiting for transfers between devices: 66 us -> 76.5 us  [broadcast(): return lax.psum(kept, axis)]
    unnamed x50 -> x105, local copies, waits for them, and re-layouts: 14.4 us -> 20.4 us
  transfers between devices with their start and end apart: 11 -> 53, of which waited for: 11 -> 14; matrix products, arithmetic and copies ran while one was open for 7% -> 9% of each run, Pallas kernels for 0% -> 0%
where the time goes in v1:
time: 675 us; the launch traced here: 665 us
  waiting for transfers between devices  417 us (62%)
  starting transfers between devices  109 us (16%)
  matrix products  55.5 us (8%)
  local copies, waits for them, and re-layouts  41.9 us (6%)
  other arithmetic  27 us (4%)
  between operations  15.1 us (2%)
    reduce_scatter x3, waiting for transfers between devices, local(): lax.psum_scatter(matmul(ancestor_inverse, lower_cols), 'col', scatter_dim...  208 us
    psum x1, waiting for transfers between devices, local(): summed = lax.psum(left_dot(lower_here, stacked), ('row', 'col'))  83.8 us
    ppermute x21, starting transfers between devices, collect(): later.append(lax.ppermute(later[-1], axis, down))  83.7 us
    psum x1, waiting for transfers between devices, broadcast(): return lax.psum(kept, axis)  76.5 us
    dot_general x11, matrix products, matmul(): return jnp.dot(left, right, precision=highest)  36 us
    all_to_all x1, waiting for transfers between devices, local(): lax.all_to_all(slotted, 'col', split_axis=1, concat_axis=1, tiled=True)  21 us
    unnamed x105, local copies, waits for them, and re-layouts  20.4 us
    dot_general x6, matrix products, left_dot(): lax.dot_general(left, right, (((0,), (0,)), ((), ())), precision=highest)  17.5 us
  transfers between devices with their start and end apart: 53, of which 14 were waited for; matrix products, arithmetic and copies ran while one was open for 9% of the time, Pallas kernels for 0%

profile of v1, /device:TPU:1, one launch (start us, length us, event | category | flops | bytes accessed | tf_op | source)
XLA Modules:
  0.0 665.4 jit_solution(3259473136085064941)
XLA Ops:
  9.3 2.1 collective-permute-start.15
  11.4 4.8 collective-permute-start.23
  16.2 4.8 collective-permute-start.8
  21.0 4.8 collective-permute-start.38
  25.8 4.8 collective-permute-start.24
  30.6 4.8 collective-permute-start.9
  35.4 4.8 collective-permute-start.39
  40.2 4.8 collective-permute-start.25
  45.0 4.8 collective-permute-start.10
  49.8 4.8 collective-permute-start.40
  54.6 4.8 collective-permute-start.26
  59.4 4.8 collective-permute-start.11
  64.2 4.8 collective-permute-start.41
  69.0 4.8 collective-permute-start.27
  73.7 4.8 collective-permute-start.12
  78.6 5.0 collective-permute-start.42
  86.4 4.8 collective-permute-start.13
  92.8 2.2 collective-permute-done.21
  95.1 4.8 collective-permute-start.29
  101.4 1.9 collective-permute-done.22
  109.1 2.4 fusion.41
  111.6 2.4 fusion.43
  115.2 2.4 fusion.39
  118.0 76.5 %all-reduce.7.cloned.1.call-done = (bf16[768,512]{1,0:T(8,128)(2,1)}, bf16[768,512]{1,0:T(8,128)(2,1)}, bf16[768,512]{1,0:T(8,128)(2,1)}) async-done(((bf16[768,512]{1,0:T(8,128)(2,1)}, bf16[768,512]{1,0:T(8,128)(2,1)}, bf16[768,512]{1,0:T(8,128)(2,1)}), (bf16[768,512]{1,0:T(8,128)(2,1)}, bf16[768,512]{1,0:T(8,128)(2,1)}, bf16[768,512]{1,0:T(8,128)(2,1)})) %all-reduce.7.cloned.1.call-update) | async-done | bytes 2359312 | tf_op jit(solution)/shard_map/psum | solution.py:24
  194.5 6.7 %convolution_bitcast_fusion.2 = f32[1536,512]{0,1:T(8,128)S(1)} fusion(bf16[768,512]{1,0:T(8,128)(2,1)} %get-tuple-element.17, f32[1536,768]{1,0:T(8,128)} %param.7), kind=kOutput, calls=%fused_computation.3 | convolution fusion | flops 7247757312 | bytes 8650752 | tf_op jit(solution)/shard_map/dot_general | solution.py:28
  201.2 2.4 copy.104
  203.6 6.7 %convolution_bitcast_fusion.1 = f32[1536,512]{0,1:T(8,128)S(1)} fusion(bf16[768,512]{1,0:T(8,128)(2,1)} %get-tuple-element.18, f32[1536,768]{1,0:T(8,128)} %param.7), kind=kOutput, calls=%fused_computation.2 | convolution fusion | flops 7247757312 | bytes 8650752 | tf_op jit(solution)/shard_map/dot_general | solution.py:28
  210.3 2.4 copy.106
  212.8 6.7 %convolution_bitcast_fusion = f32[1536,512]{0,1:T(8,128)S(1)} fusion(bf16[768,512]{1,0:T(8,128)(2,1)} %get-tuple-element.16, f32[1536,768]{1,0:T(8,128)} %param.7), kind=kOutput, calls=%fused_computation.1 | convolution fusion | flops 7247757312 | bytes 8650752 | tf_op jit(solution)/shard_map/dot_general | solution.py:28
  219.5 2.4 copy.108
  222.1 57.4 %reduce-scatter.10.cloned.1.call-done = f32[96,512]{1,0:T(8,128)} async-done(((f32[1536,512]{1,0:T(8,128)}), f32[96,512]{1,0:T(8,128)}) %reduce-scatter.10.cloned.1.call-update) | async-done | bytes 196624 | tf_op jit(solution)/shard_map/reduce_scatter | solution.py:60
  281.2 76.8 %reduce-scatter.12.cloned.1.call-done = f32[96,512]{1,0:T(8,128)} async-done(((f32[1536,512]{1,0:T(8,128)}), f32[96,512]{1,0:T(8,128)}) %reduce-scatter.12.cloned.1.call-update) | async-done | bytes 196624 | tf_op jit(solution)/shard_map/reduce_scatter | solution.py:60
  358.0 1.8 fusion.5
  359.8 3.3 fusion.51
  363.1 73.7 %reduce-scatter.14.cloned.1.call-done = f32[96,512]{1,0:T(8,128)} async-done(((f32[1536,512]{1,0:T(8,128)}), f32[96,512]{1,0:T(8,128)}) %reduce-scatter.14.cloned.1.call-update) | async-done | bytes 196624 | tf_op jit(solution)/shard_map/reduce_scatter | solution.py:60
  439.4 3.1 fusion.44
  450.3 6.6 all-to-all-start
  456.9 15.7 %all-to-all-done = f32[3,8,12,512]{3,2,0,1:T(8,128)} async-done(((f32[3,8,12,512]{3,2,0,1:T(8,128)}), f32[3,8,12,512]{3,2,0,1:T(8,128)}, u32[]{:S(2)}, u32[]{:S(2)}) %all-to-all-start) | async-done | bytes 589856 | tf_op jit(solution)/shard_map/all_to_all | solution.py:93
  472.6 2.1 convolution_bitcast_fusion.3
  474.7 1.9 copy.80
  476.6 4.7 all-to-all-start.1
  481.3 21.0 %all-to-all-done.1 = f32[3,16,12,512]{3,2,0,1:T(8,128)} async-done(((f32[3,16,12,512]{3,2,0,1:T(8,128)}), f32[3,16,12,512]{3,2,0,1:T(8,128)}, u32[]{:S(2)}, u32[]{:S(2)}) %all-to-all-start.1) | async-done | bytes 1179680 | tf_op jit(solution)/shard_map/all_to_all | solution.py:99
  502.3 2.1 constant_dynamic-slice_fusion
  504.4 9.1 %all-to-all-start.2 = ((f32[3,8,12,512]{3,2,0,1:T(8,128)}), f32[3,8,12,512]{3,2,0,1:T(8,128)}, u32[]{:S(2)}, u32[]{:S(2)}) async-start(f32[3,8,12,512]{3,2,0,1:T(8,128)} %constant_dynamic-slice_fusion), calls=%async_computation.2 | async-start | bytes 1572864 | tf_op jit(solution)/shard_map/all_to_all | solution.py:101
  513.5 2.3 slice.71
  515.9 2.5 copy.110
  520.2 5.7 all-to-all-done.2
  525.9 2.2 copy.81
  528.1 2.0 reshape.46
  530.1 83.8 %all-reduce.5.cloned.1.call-done = (f32[512,1536]{1,0:T(8,128)}, f32[512,512]{1,0:T(8,128)}, f32[512,1024]{0,1:T(8,128)}) async-done(((f32[512,1536]{1,0:T(8,128)}, f32[512,512]{1,0:T(8,128)}, f32[512,1024]{0,1:T(8,128)}), (f32[512,1536]{1,0:T(8,128)}, f32[512,512]{1,0:T(8,128)}, f32[512,1024]{0,1:T(8,128)})) %all-reduce.5.cloned.1.call-update) | async-done | bytes 6291472 | tf_op jit(solution)/shard_map/psum | solution.py:69
  614.0 3.8 bitcast_subtract_fusion.7
  617.8 1.9 fusion.14
  619.7 1.9 fusion.18
  621.6 1.9 fusion.20
  623.8 2.0 fusion.3
  625.8 2.2 fusion.12
  628.1 3.1 fusion.2
  631.2 2.3 fusion.7
  633.5 2.3 fusion.66
  635.8 2.6 copy.85
  638.4 3.8 maximum_bitcast_fusion.1
  642.2 3.5 copy.95
  645.8 4.3 fusion.1
  653.5 4.9 pad_maximum_fusion
  (201 shorter events, 33.3 us)
Async XLA Ops:
  7.2 187.3 %all-reduce.7.cloned.1.call-start = ((), (), s32[]{:S(2)}) async-start(), calls=%async_computation.10 | async-start | bytes 4718592 | tf_op jit(solution)/shard_map/psum | solution.py:24
  9.2 99.7 %copy-start.21 = (bf16[96,512]{1,0:T(8,128)(2,1)}, bf16[96,512]{1,0:T(8,128)(2,1)S(1)}, u32[]{:S(2)}) copy-start(bf16[96,512]{1,0:T(8,128)(2,1)S(1)} %get-tuple-element.23) | copy-start | bytes 294916
  9.2 99.7 %copy-start.22 = (bf16[96,512]{1,0:T(8,128)(2,1)}, bf16[96,512]{1,0:T(8,128)(2,1)S(1)}, u32[]{:S(2)}) copy-start(bf16[96,512]{1,0:T(8,128)(2,1)S(1)} %get-tuple-element.24) | copy-start | bytes 294916
  9.3 105.8 %copy-start.24 = (bf16[96,512]{1,0:T(8,128)(2,1)}, bf16[96,512]{1,0:T(8,128)(2,1)S(1)}, u32[]{:S(2)}) copy-start(bf16[96,512]{1,0:T(8,128)(2,1)S(1)} %get-tuple-element.25) | copy-start | bytes 294916
  9.3 11.7 %collective-permute-start.15 = (bf16[96,512]{1,0:T(8,128)(2,1)S(1)}, bf16[96,512]{1,0:T(8,128)(2,1)S(1)}, u32[]{:S(2)}, u32[]{:S(2)}) collective-permute-start(bf16[96,512]{1,0:T(8,128)(2,1)S(1)} %get-tuple-element.23), channel_id=1, source_target_pairs={{0,1},{1,2},{2,3},{3,4},{4,5},{5,6},{6,7},{7,8},{8,9},{9,10},{10,1... | collective-permute-start | bytes 294920 | tf_op jit(solution)/shard_map/ppermute | solution.py:15
  11.4 14.4 %collective-permute-start.23 = (bf16[96,512]{1,0:T(8,128)(2,1)S(1)}, bf16[96,512]{1,0:T(8,128)(2,1)S(1)}, u32[]{:S(2)}, u32[]{:S(2)}) collective-permute-start(bf16[96,512]{1,0:T(8,128)(2,1)S(1)} %get-tuple-element.23), channel_id=1, source_target_pairs={{0,15},{1,0},{2,1},{3,2},{4,3},{5,4},{6,5},{7,6},{8,7},{9,8},{10,9... | collective-permute-start | bytes 294920 | tf_op jit(solution)/shard_map/ppermute | solution.py:17
  16.2 9.6 %collective-permute-start = (bf16[96,512]{1,0:T(8,128)(2,1)S(1)}, bf16[96,512]{1,0:T(8,128)(2,1)S(1)}, u32[]{:S(2)}, u32[]{:S(2)}) collective-permute-start(bf16[96,512]{1,0:T(8,128)(2,1)S(1)} %get-tuple-element.24), channel_id=1, source_target_pairs={{0,1},{1,2},{2,3},{3,4},{4,5},{5,6},{6,7},{7,8},{8,9},{9,10},{10,1... | collective-permute-start | bytes 294920 | tf_op jit(solution)/shard_map/ppermute | solution.py:15
  16.2 14.4 %collective-permute-start.8 = (bf16[96,512]{1,0:T(8,128)(2,1)S(1)}, bf16[96,512]{1,0:T(8,128)(2,1)S(1)}, u32[]{:S(2)}, u32[]{:S(2)}) collective-permute-start(bf16[96,512]{1,0:T(8,128)(2,1)S(1)} %get-tuple-element.24), channel_id=1, source_target_pairs={{0,15},{1,0},{2,1},{3,2},{4,3},{5,4},{6,5},{7,6},{8,7},{9,8},{10,9... | collective-permute-start | bytes 294920 | tf_op jit(solution)/shard_map/ppermute | solution.py:17
  21.0 9.6 %collective-permute-start.30 = (bf16[96,512]{1,0:T(8,128)(2,1)S(1)}, bf16[96,512]{1,0:T(8,128)(2,1)S(1)}, u32[]{:S(2)}, u32[]{:S(2)}) collective-permute-start(bf16[96,512]{1,0:T(8,128)(2,1)S(1)} %get-tuple-element.25), channel_id=1, source_target_pairs={{0,1},{1,2},{2,3},{3,4},{4,5},{5,6},{6,7},{7,8},{8,9},{9,10},{10,1... | collective-permute-start | bytes 294920 | tf_op jit(solution)/shard_map/ppermute | solution.py:15
  21.0 14.4 %collective-permute-start.38 = (bf16[96,512]{1,0:T(8,128)(2,1)S(1)}, bf16[96,512]{1,0:T(8,128)(2,1)S(1)}, u32[]{:S(2)}, u32[]{:S(2)}) collective-permute-start(bf16[96,512]{1,0:T(8,128)(2,1)S(1)} %get-tuple-element.25), channel_id=1, source_target_pairs={{0,15},{1,0},{2,1},{3,2},{4,3},{5,4},{6,5},{7,6},{8,7},{9,8},{10,9... | collective-permute-start | bytes 294920 | tf_op jit(solution)/shard_map/ppermute | solution.py:17
  25.8 9.6 %collective-permute-start.16 = (bf16[96,512]{1,0:T(8,128)(2,1)S(1)}, bf16[96,512]{1,0:T(8,128)(2,1)S(1)}, u32[]{:S(2)}, u32[]{:S(2)}) collective-permute-start(bf16[96,512]{1,0:T(8,128)(2,1)S(1)} %collective-permute-done.15), channel_id=1, source_target_pairs={{0,1},{1,2},{2,3},{3,4},{4,5},{5,6},{6,7},{7,8},{8,9},{9,10},{10,1... | collective-permute-start | bytes 294920 | tf_op jit(solution)/shard_map/ppermute | solution.py:15
  25.8 14.4 %collective-permute-start.24 = (bf16[96,512]{1,0:T(8,128)(2,1)S(1)}, bf16[96,512]{1,0:T(8,128)(2,1)S(1)}, u32[]{:S(2)}, u32[]{:S(2)}) collective-permute-start(bf16[96,512]{1,0:T(8,128)(2,1)S(1)} %collective-permute-done.23), channel_id=1, source_target_pairs={{0,15},{1,0},{2,1},{3,2},{4,3},{5,4},{6,5},{7,6},{8,7},{9,8},{10,9... | collective-permute-start | bytes 294920 | tf_op jit(solution)/shard_map/ppermute | solution.py:17
  30.6 9.6 %collective-permute-start.1 = (bf16[96,512]{1,0:T(8,128)(2,1)S(1)}, bf16[96,512]{1,0:T(8,128)(2,1)S(1)}, u32[]{:S(2)}, u32[]{:S(2)}) collective-permute-start(bf16[96,512]{1,0:T(8,128)(2,1)S(1)} %collective-permute-done), channel_id=1, source_target_pairs={{0,1},{1,2},{2,3},{3,4},{4,5},{5,6},{6,7},{7,8},{8,9},{9,10},{10,1... | collective-permute-start | bytes 294920 | tf_op jit(solution)/shard_map/ppermute | solution.py:15
  30.6 14.4 %collective-permute-start.9 = (bf16[96,512]{1,0:T(8,128)(2,1)S(1)}, bf16[96,512]{1,0:T(8,128)(2,1)S(1)}, u32[]{:S(2)}, u32[]{:S(2)}) collective-permute-start(bf16[96,512]{1,0:T(8,128)(2,1)S(1)} %collective-permute-done.8), channel_id=1, source_target_pairs={{0,15},{1,0},{2,1},{3,2},{4,3},{5,4},{6,5},{7,6},{8,7},{9,8},{10,9... | collective-permute-start | bytes 294920 | tf_op jit(solution)/shard_map/ppermute | solution.py:17
  35.4 9.6 %collective-permute-start.31 = (bf16[96,512]{1,0:T(8,128)(2,1)S(1)}, bf16[96,512]{1,0:T(8,128)(2,1)S(1)}, u32[]{:S(2)}, u32[]{:S(2)}) collective-permute-start(bf16[96,512]{1,0:T(8,128)(2,1)S(1)} %collective-permute-done.30), channel_id=1, source_target_pairs={{0,1},{1,2},{2,3},{3,4},{4,5},{5,6},{6,7},{7,8},{8,9},{9,10},{10,1... | collective-permute-start | bytes 294920 | tf_op jit(solution)/shard_map/ppermute | solution.py:15
  35.4 14.4 %collective-permute-start.39 = (bf16[96,512]{1,0:T(8,128)(2,1)S(1)}, bf16[96,512]{1,0:T(8,128)(2,1)S(1)}, u32[]{:S(2)}, u32[]{:S(2)}) collective-permute-start(bf16[96,512]{1,0:T(8,128)(2,1)S(1)} %collective-permute-done.38), channel_id=1, source_target_pairs={{0,15},{1,0},{2,1},{3,2},{4,3},{5,4},{6,5},{7,6},{8,7},{9,8},{10,9... | collective-permute-start | bytes 294920 | tf_op jit(solution)/shard_map/ppermute | solution.py:17
  40.2 9.6 %collective-permute-start.17 = (bf16[96,512]{1,0:T(8,128)(2,1)S(1)}, bf16[96,512]{1,0:T(8,128)(2,1)S(1)}, u32[]{:S(2)}, u32[]{:S(2)}) collective-permute-start(bf16[96,512]{1,0:T(8,128)(2,1)S(1)} %collective-permute-done.16), channel_id=1, source_target_pairs={{0,1},{1,2},{2,3},{3,4},{4,5},{5,6},{6,7},{7,8},{8,9},{9,10},{10,1... | collective-permute-start | bytes 294920 | tf_op jit(solution)/shard_map/ppermute | solution.py:15
  40.2 14.4 %collective-permute-start.25 = (bf16[96,512]{1,0:T(8,128)(2,1)S(1)}, bf16[96,512]{1,0:T(8,128)(2,1)S(1)}, u32[]{:S(2)}, u32[]{:S(2)}) collective-permute-start(bf16[96,512]{1,0:T(8,128)(2,1)S(1)} %collective-permute-done.24), channel_id=1, source_target_pairs={{0,15},{1,0},{2,1},{3,2},{4,3},{5,4},{6,5},{7,6},{8,7},{9,8},{10,9... | collective-permute-start | bytes 294920 | tf_op jit(solution)/shard_map/ppermute | solution.py:17
  45.0 9.6 %collective-permute-start.2 = (bf16[96,512]{1,0:T(8,128)(2,1)S(1)}, bf16[96,512]{1,0:T(8,128)(2,1)S(1)}, u32[]{:S(2)}, u32[]{:S(2)}) collective-permute-start(bf16[96,512]{1,0:T(8,128)(2,1)S(1)} %collective-permute-done.1), channel_id=1, source_target_pairs={{0,1},{1,2},{2,3},{3,4},{4,5},{5,6},{6,7},{7,8},{8,9},{9,10},{10,1... | collective-permute-start | bytes 294920 | tf_op jit(solution)/shard_map/ppermute | solution.py:15
  45.0 14.4 %collective-permute-start.10 = (bf16[96,512]{1,0:T(8,128)(2,1)S(1)}, bf16[96,512]{1,0:T(8,128)(2,1)S(1)}, u32[]{:S(2)}, u32[]{:S(2)}) collective-permute-start(bf16[96,512]{1,0:T(8,128)(2,1)S(1)} %collective-permute-done.9), channel_id=1, source_target_pairs={{0,15},{1,0},{2,1},{3,2},{4,3},{5,4},{6,5},{7,6},{8,7},{9,8},{10,9... | collective-permute-start | bytes 294920 | tf_op jit(solution)/shard_map/ppermute | solution.py:17
  49.8 9.6 %collective-permute-start.32 = (bf16[96,512]{1,0:T(8,128)(2,1)S(1)}, bf16[96,512]{1,0:T(8,128)(2,1)S(1)}, u32[]{:S(2)}, u32[]{:S(2)}) collective-permute-start(bf16[96,512]{1,0:T(8,128)(2,1)S(1)} %collective-permute-done.31), channel_id=1, source_target_pairs={{0,1},{1,2},{2,3},{3,4},{4,5},{5,6},{6,7},{7,8},{8,9},{9,10},{10,1... | collective-permute-start | bytes 294920 | tf_op jit(solution)/shard_map/ppermute | solution.py:15
  49.8 14.4 %collective-permute-start.40 = (bf16[96,512]{1,0:T(8,128)(2,1)S(1)}, bf16[96,512]{1,0:T(8,128)(2,1)S(1)}, u32[]{:S(2)}, u32[]{:S(2)}) collective-permute-start(bf16[96,512]{1,0:T(8,128)(2,1)S(1)} %collective-permute-done.39), channel_id=1, source_target_pairs={{0,15},{1,0},{2,1},{3,2},{4,3},{5,4},{6,5},{7,6},{8,7},{9,8},{10,9... | collective-permute-start | bytes 294920 | tf_op jit(solution)/shard_map/ppermute | solution.py:17
  54.5 9.6 %collective-permute-start.18 = (bf16[96,512]{1,0:T(8,128)(2,1)S(1)}, bf16[96,512]{1,0:T(8,128)(2,1)S(1)}, u32[]{:S(2)}, u32[]{:S(2)}) collective-permute-start(bf16[96,512]{1,0:T(8,128)(2,1)S(1)} %collective-permute-done.17), channel_id=1, source_target_pairs={{0,1},{1,2},{2,3},{3,4},{4,5},{5,6},{6,7},{7,8},{8,9},{9,10},{10,1... | collective-permute-start | bytes 294920 | tf_op jit(solution)/shard_map/ppermute | solution.py:15
  54.6 14.4 %collective-permute-start.26 = (bf16[96,512]{1,0:T(8,128)(2,1)S(1)}, bf16[96,512]{1,0:T(8,128)(2,1)S(1)}, u32[]{:S(2)}, u32[]{:S(2)}) collective-permute-start(bf16[96,512]{1,0:T(8,128)(2,1)S(1)} %collective-permute-done.25), channel_id=1, source_target_pairs={{0,15},{1,0},{2,1},{3,2},{4,3},{5,4},{6,5},{7,6},{8,7},{9,8},{10,9... | collective-permute-start | bytes 294920 | tf_op jit(solution)/shard_map/ppermute | solution.py:17
  59.4 9.6 %collective-permute-start.3 = (bf16[96,512]{1,0:T(8,128)(2,1)S(1)}, bf16[96,512]{1,0:T(8,128)(2,1)S(1)}, u32[]{:S(2)}, u32[]{:S(2)}) collective-permute-start(bf16[96,512]{1,0:T(8,128)(2,1)S(1)} %collective-permute-done.2), channel_id=1, source_target_pairs={{0,1},{1,2},{2,3},{3,4},{4,5},{5,6},{6,7},{7,8},{8,9},{9,10},{10,1... | collective-permute-start | bytes 294920 | tf_op jit(solution)/shard_map/ppermute | solution.py:15
  59.4 14.4 %collective-permute-start.11 = (bf16[96,512]{1,0:T(8,128)(2,1)S(1)}, bf16[96,512]{1,0:T(8,128)(2,1)S(1)}, u32[]{:S(2)}, u32[]{:S(2)}) collective-permute-start(bf16[96,512]{1,0:T(8,128)(2,1)S(1)} %collective-permute-done.10), channel_id=1, source_target_pairs={{0,15},{1,0},{2,1},{3,2},{4,3},{5,4},{6,5},{7,6},{8,7},{9,8},{10,9... | collective-permute-start | bytes 294920 | tf_op jit(solution)/shard_map/ppermute | solution.py:17
  64.1 9.6 %collective-permute-start.33 = (bf16[96,512]{1,0:T(8,128)(2,1)S(1)}, bf16[96,512]{1,0:T(8,128)(2,1)S(1)}, u32[]{:S(2)}, u32[]{:S(2)}) collective-permute-start(bf16[96,512]{1,0:T(8,128)(2,1)S(1)} %collective-permute-done.32), channel_id=1, source_target_pairs={{0,1},{1,2},{2,3},{3,4},{4,5},{5,6},{6,7},{7,8},{8,9},{9,10},{10,1... | collective-permute-start | bytes 294920 | tf_op jit(solution)/shard_map/ppermute | solution.py:15
  64.2 14.4 %collective-permute-start.41 = (bf16[96,512]{1,0:T(8,128)(2,1)S(1)}, bf16[96,512]{1,0:T(8,128)(2,1)S(1)}, u32[]{:S(2)}, u32[]{:S(2)}) collective-permute-start(bf16[96,512]{1,0:T(8,128)(2,1)S(1)} %collective-permute-done.40), channel_id=1, source_target_pairs={{0,15},{1,0},{2,1},{3,2},{4,3},{5,4},{6,5},{7,6},{8,7},{9,8},{10,9... | collective-permute-start | bytes 294920 | tf_op jit(solution)/shard_map/ppermute | solution.py:17
  68.9 9.6 %collective-permute-start.19 = (bf16[96,512]{1,0:T(8,128)(2,1)S(1)}, bf16[96,512]{1,0:T(8,128)(2,1)S(1)}, u32[]{:S(2)}, u32[]{:S(2)}) collective-permute-start(bf16[96,512]{1,0:T(8,128)(2,1)S(1)} %collective-permute-done.18), channel_id=1, source_target_pairs={{0,1},{1,2},{2,3},{3,4},{4,5},{5,6},{6,7},{7,8},{8,9},{9,10},{10,1... | collective-permute-start | bytes 294920 | tf_op jit(solution)/shard_map/ppermute | solution.py:15
  69.0 9.7 %collective-permute-start.27 = (bf16[96,512]{1,0:T(8,128)(2,1)S(1)}, bf16[96,512]{1,0:T(8,128)(2,1)S(1)}, u32[]{:S(2)}, u32[]{:S(2)}) collective-permute-start(bf16[96,512]{1,0:T(8,128)(2,1)S(1)} %collective-permute-done.26), channel_id=1, source_target_pairs={{0,15},{1,0},{2,1},{3,2},{4,3},{5,4},{6,5},{7,6},{8,7},{9,8},{10,9... | collective-permute-start | bytes 294920 | tf_op jit(solution)/shard_map/ppermute | solution.py:17
  73.7 9.9 %collective-permute-start.4 = (bf16[96,512]{1,0:T(8,128)(2,1)S(1)}, bf16[96,512]{1,0:T(8,128)(2,1)S(1)}, u32[]{:S(2)}, u32[]{:S(2)}) collective-permute-start(bf16[96,512]{1,0:T(8,128)(2,1)S(1)} %collective-permute-done.3), channel_id=1, source_target_pairs={{0,1},{1,2},{2,3},{3,4},{4,5},{5,6},{6,7},{7,8},{8,9},{9,10},{10,1... | collective-permute-start | bytes 294920 | tf_op jit(solution)/shard_map/ppermute | solution.py:15
  73.7 11.2 %collective-permute-start.12 = (bf16[96,512]{1,0:T(8,128)(2,1)S(1)}, bf16[96,512]{1,0:T(8,128)(2,1)S(1)}, u32[]{:S(2)}, u32[]{:S(2)}) collective-permute-start(bf16[96,512]{1,0:T(8,128)(2,1)S(1)} %collective-permute-done.11), channel_id=1, source_target_pairs={{0,15},{1,0},{2,1},{3,2},{4,3},{5,4},{6,5},{7,6},{8,7},{9,8},{10,9... | collective-permute-start | bytes 294920 | tf_op jit(solution)/shard_map/ppermute | solution.py:17
  78.5 6.8 %collective-permute-start.34 = (bf16[96,512]{1,0:T(8,128)(2,1)S(1)}, bf16[96,512]{1,0:T(8,128)(2,1)S(1)}, u32[]{:S(2)}, u32[]{:S(2)}) collective-permute-start(bf16[96,512]{1,0:T(8,128)(2,1)S(1)} %collective-permute-done.33), channel_id=1, source_target_pairs={{0,1},{1,2},{2,3},{3,4},{4,5},{5,6},{6,7},{7,8},{8,9},{9,10},{10,1... | collective-permute-start | bytes 294920 | tf_op jit(solution)/shard_map/ppermute | solution.py:15
  78.5 12.6 %copy-start.26 = (bf16[96,512]{1,0:T(8,128)(2,1)}, bf16[96,512]{1,0:T(8,128)(2,1)S(1)}, u32[]{:S(2)}) copy-start(bf16[96,512]{1,0:T(8,128)(2,1)S(1)} %collective-permute-done.19) | copy-start | bytes 294916
  78.6 7.8 %collective-permute-start.20 = (bf16[96,512]{1,0:T(8,128)(2,1)S(1)}, bf16[96,512]{1,0:T(8,128)(2,1)S(1)}, u32[]{:S(2)}, u32[]{:S(2)}) collective-permute-start(bf16[96,512]{1,0:T(8,128)(2,1)S(1)} %collective-permute-done.19), channel_id=1, source_target_pairs={{0,1},{1,2},{2,3},{3,4},{4,5},{5,6},{6,7},{7,8},{8,9},{9,10},{10,1... | collective-permute-start | bytes 294920 | tf_op jit(solution)/shard_map/ppermute | solution.py:15
  78.6 7.7 %collective-permute-start.42 = (bf16[96,512]{1,0:T(8,128)(2,1)S(1)}, bf16[96,512]{1,0:T(8,128)(2,1)S(1)}, u32[]{:S(2)}, u32[]{:S(2)}) collective-permute-start(bf16[96,512]{1,0:T(8,128)(2,1)S(1)} %collective-permute-done.41), channel_id=1, source_target_pairs={{0,15},{1,0},{2,1},{3,2},{4,3},{5,4},{6,5},{7,6},{8,7},{9,8},{10,9... | collective-permute-start | bytes 294920 | tf_op jit(solution)/shard_map/ppermute | solution.py:17
  83.6 7.5 %collective-permute-start.28 = (bf16[96,512]{1,0:T(8,128)(2,1)S(1)}, bf16[96,512]{1,0:T(8,128)(2,1)S(1)}, u32[]{:S(2)}, u32[]{:S(2)}) collective-permute-start(bf16[96,512]{1,0:T(8,128)(2,1)S(1)} %collective-permute-done.27), channel_id=1, source_target_pairs={{0,15},{1,0},{2,1},{3,2},{4,3},{5,4},{6,5},{7,6},{8,7},{9,8},{10,9... | collective-permute-start | bytes 294920 | tf_op jit(solution)/shard_map/ppermute | solution.py:17
  85.0 6.9 %collective-permute-start.5 = (bf16[96,512]{1,0:T(8,128)(2,1)S(1)}, bf16[96,512]{1,0:T(8,128)(2,1)}, u32[]{:S(2)}, u32[]{:S(2)}) collective-permute-start(bf16[96,512]{1,0:T(8,128)(2,1)S(1)} %collective-permute-done.4), channel_id=1, source_target_pairs={{0,1},{1,2},{2,3},{3,4},{4,5},{5,6},{6,7},{7,8},{8,9},{9,10},{10,1... | collective-permute-start | bytes 294920 | tf_op jit(solution)/shard_map/ppermute | solution.py:15
  85.3 7.5 %collective-permute-start.35 = (bf16[96,512]{1,0:T(8,128)(2,1)S(1)}, bf16[96,512]{1,0:T(8,128)(2,1)S(1)}, u32[]{:S(2)}, u32[]{:S(2)}) collective-permute-start(bf16[96,512]{1,0:T(8,128)(2,1)S(1)} %collective-permute-done.34), channel_id=1, source_target_pairs={{0,1},{1,2},{2,3},{3,4},{4,5},{5,6},{6,7},{7,8},{8,9},{9,10},{10,1... | collective-permute-start | bytes 294920 | tf_op jit(solution)/shard_map/ppermute | solution.py:15
  86.4 6.5 copy-start.27
  86.4 8.7 %collective-permute-start.21 = (bf16[96,512]{1,0:T(8,128)(2,1)S(1)}, bf16[96,512]{1,0:T(8,128)(2,1)}, u32[]{:S(2)}, u32[]{:S(2)}) collective-permute-start(bf16[96,512]{1,0:T(8,128)(2,1)S(1)} %collective-permute-done.20), channel_id=1, source_target_pairs={{0,1},{1,2},{2,3},{3,4},{4,5},{5,6},{6,7},{7,8},{8,9},{9,10},{10,1... | collective-permute-start | bytes 294920 | tf_op jit(solution)/shard_map/ppermute | solution.py:15
  86.4 8.7 %collective-permute-start.13 = (bf16[96,512]{1,0:T(8,128)(2,1)S(1)}, bf16[96,512]{1,0:T(8,128)(2,1)S(1)}, u32[]{:S(2)}, u32[]{:S(2)}) collective-permute-start(bf16[96,512]{1,0:T(8,128)(2,1)S(1)} %collective-permute-done.12), channel_id=1, source_target_pairs={{0,15},{1,0},{2,1},{3,2},{4,3},{5,4},{6,5},{7,6},{8,7},{9,8},{10,9... | collective-permute-start | bytes 294920 | tf_op jit(solution)/shard_map/ppermute | solution.py:17
  91.2 8.7 %collective-permute-start.43 = (bf16[96,512]{1,0:T(8,128)(2,1)S(1)}, bf16[96,512]{1,0:T(8,128)(2,1)S(1)}, u32[]{:S(2)}, u32[]{:S(2)}) collective-permute-start(bf16[96,512]{1,0:T(8,128)(2,1)S(1)} %collective-permute-done.42), channel_id=1, source_target_pairs={{0,15},{1,0},{2,1},{3,2},{4,3},{5,4},{6,5},{7,6},{8,7},{9,8},{10,9... | collective-permute-start | bytes 294920 | tf_op jit(solution)/shard_map/ppermute | solution.py:17
  91.9 8.0 %collective-permute-start.6 = (bf16[96,512]{1,0:T(8,128)(2,1)}, bf16[96,512]{1,0:T(8,128)(2,1)}, u32[]{:S(2)}, u32[]{:S(2)}) collective-permute-start(bf16[96,512]{1,0:T(8,128)(2,1)} %collective-permute-done.5), channel_id=1, source_target_pairs={{0,1},{1,2},{2,3},{3,4},{4,5},{5,6},{6,7},{7,8},{8,9},{9,10},{10,1... | collective-permute-start | bytes 294920 | tf_op jit(solution)/shard_map/ppermute | solution.py:15
  92.8 7.2 %collective-permute-start.36 = (bf16[96,512]{1,0:T(8,128)(2,1)S(1)}, bf16[96,512]{1,0:T(8,128)(2,1)}, u32[]{:S(2)}, u32[]{:S(2)}) collective-permute-start(bf16[96,512]{1,0:T(8,128)(2,1)S(1)} %collective-permute-done.35), channel_id=1, source_target_pairs={{0,1},{1,2},{2,3},{3,4},{4,5},{5,6},{6,7},{7,8},{8,9},{9,10},{10,1... | collective-permute-start | bytes 294920 | tf_op jit(solution)/shard_map/ppermute | solution.py:15
  95.1 8.3 %collective-permute-start.22 = (bf16[96,512]{1,0:T(8,128)(2,1)}, bf16[96,512]{1,0:T(8,128)(2,1)}, u32[]{:S(2)}, u32[]{:S(2)}) collective-permute-start(bf16[96,512]{1,0:T(8,128)(2,1)} %collective-permute-done.21), channel_id=1, source_target_pairs={{0,1},{1,2},{2,3},{3,4},{4,5},{5,6},{6,7},{7,8},{8,9},{9,10},{10,1... | collective-permute-start | bytes 294920 | tf_op jit(solution)/shard_map/ppermute | solution.py:15
  95.1 14.0 %collective-permute-start.29 = (bf16[96,512]{1,0:T(8,128)(2,1)S(1)}, bf16[96,512]{1,0:T(8,128)(2,1)S(1)}, u32[]{:S(2)}, u32[]{:S(2)}) collective-permute-start(bf16[96,512]{1,0:T(8,128)(2,1)S(1)} %collective-permute-done.28), channel_id=1, source_target_pairs={{0,15},{1,0},{2,1},{3,2},{4,3},{5,4},{6,5},{7,6},{8,7},{9,8},{10,9... | collective-permute-start | bytes 294920 | tf_op jit(solution)/shard_map/ppermute | solution.py:17
  99.8 11.7 %collective-permute-start.14 = (bf16[96,512]{1,0:T(8,128)(2,1)S(1)}, bf16[96,512]{1,0:T(8,128)(2,1)S(1)}, u32[]{:S(2)}, u32[]{:S(2)}) collective-permute-start(bf16[96,512]{1,0:T(8,128)(2,1)S(1)} %collective-permute-done.13), channel_id=1, source_target_pairs={{0,15},{1,0},{2,1},{3,2},{4,3},{5,4},{6,5},{7,6},{8,7},{9,8},{10,9... | collective-permute-start | bytes 294920 | tf_op jit(solution)/shard_map/ppermute | solution.py:17
  99.9 15.2 %collective-permute-start.44 = (bf16[96,512]{1,0:T(8,128)(2,1)S(1)}, bf16[96,512]{1,0:T(8,128)(2,1)S(1)}, u32[]{:S(2)}, u32[]{:S(2)}) collective-permute-start(bf16[96,512]{1,0:T(8,128)(2,1)S(1)} %collective-permute-done.43), channel_id=1, source_target_pairs={{0,15},{1,0},{2,1},{3,2},{4,3},{5,4},{6,5},{7,6},{8,7},{9,8},{10,9... | collective-permute-start | bytes 294920 | tf_op jit(solution)/shard_map/ppermute | solution.py:17
  100.0 7.0 %collective-permute-start.7 = (bf16[96,512]{1,0:T(8,128)(2,1)}, bf16[96,512]{1,0:T(8,128)(2,1)S(1)}, u32[]{:S(2)}, u32[]{:S(2)}) collective-permute-start(bf16[96,512]{1,0:T(8,128)(2,1)} %collective-permute-done.6), channel_id=1, source_target_pairs={{0,1},{1,2},{2,3},{3,4},{4,5},{5,6},{6,7},{7,8},{8,9},{9,10},{10,1... | collective-permute-start | bytes 294920 | tf_op jit(solution)/shard_map/ppermute | solution.py:15
  103.3 10.7 %collective-permute-start.37 = (bf16[96,512]{1,0:T(8,128)(2,1)}, bf16[96,512]{1,0:T(8,128)(2,1)S(1)}, u32[]{:S(2)}, u32[]{:S(2)}) collective-permute-start(bf16[96,512]{1,0:T(8,128)(2,1)} %collective-permute-done.36), channel_id=1, source_target_pairs={{0,1},{1,2},{2,3},{3,4},{4,5},{5,6},{6,7},{7,8},{8,9},{9,10},{10,1... | collective-permute-start | bytes 294920 | tf_op jit(solution)/shard_map/ppermute | solution.py:15
  117.6 161.9 %reduce-scatter.10.cloned.1.call-start = ((), (), s32[]{:S(2)}) async-start(), calls=%async_computation.6 | async-start | bytes 3342336 | tf_op jit(solution)/shard_map/reduce_scatter | solution.py:60
  203.6 154.4 %reduce-scatter.12.cloned.1.call-start = ((), (), s32[]{:S(2)}) async-start(), calls=%async_computation.7 | async-start | bytes 3342336 | tf_op jit(solution)/shard_map/reduce_scatter | solution.py:60
  212.7 224.1 %reduce-scatter.14.cloned.1.call-start = ((), (), s32[]{:S(2)}) async-start(), calls=%async_computation.8 | async-start | bytes 3342336 | tf_op jit(solution)/shard_map/reduce_scatter | solution.py:60
  221.9 136.1 %copy-start = (f32[3,512,512]{2,1,0:T(8,128)S(1)}, f32[3,512,512]{2,1,0:T(8,128)}, u32[]{:S(2)}) copy-start(f32[3,512,512]{2,1,0:T(8,128)} %param.9) | copy-start | bytes 9437188
  221.9 392.1 %all-reduce.5.cloned.1.call-start = ((), (), s32[]{:S(2)}) async-start(), calls=%async_computation.9 | async-start | bytes 12582912 | tf_op jit(solution)/shard_map/psum | solution.py:69
  359.8 77.1 %copy-start.16 = (f32[96,512]{1,0:T(8,128)S(1)}, f32[96,512]{1,0:T(8,128)}, u32[]{:S(2)}) copy-start(f32[96,512]{1,0:T(8,128)} %reduce-scatter.10.cloned.1.call-done) | copy-start | bytes 589828
  450.3 22.4 %all-to-all-start = ((f32[3,8,12,512]{3,2,0,1:T(8,128)}), f32[3,8,12,512]{3,2,0,1:T(8,128)}, u32[]{:S(2)}, u32[]{:S(2)}) async-start(f32[3,8,12,512]{3,2,0,1:T(8,128)} %copy.78), calls=%async_computation | async-start | bytes 1572864 | tf_op jit(solution)/shard_map/all_to_all | solution.py:93
  476.6 25.7 %all-to-all-start.1 = ((f32[3,16,12,512]{3,2,0,1:T(8,128)}), f32[3,16,12,512]{3,2,0,1:T(8,128)}, u32[]{:S(2)}, u32[]{:S(2)}) async-start(f32[3,16,12,512]{3,2,0,1:T(8,128)} %copy.80), calls=%async_computation.1 | async-start | bytes 3145728 | tf_op jit(solution)/shard_map/all_to_all | solution.py:99
  504.4 21.5 %all-to-all-start.2 = ((f32[3,8,12,512]{3,2,0,1:T(8,128)}), f32[3,8,12,512]{3,2,0,1:T(8,128)}, u32[]{:S(2)}, u32[]{:S(2)}) async-start(f32[3,8,12,512]{3,2,0,1:T(8,128)} %constant_dynamic-slice_fusion), calls=%async_computation.2 | async-start | bytes 1572864 | tf_op jit(solution)/shard_map/all_to_all | solution.py:101
  617.7 5.8 copy-start.1
  621.6 11.9 %copy-start.3 = (f32[512,512]{0,1:T(8,128)}, f32[512,512]{0,1:T(8,128)S(1)}, u32[]{:S(2)}) copy-start(f32[512,512]{0,1:T(8,128)S(1)} %fusion.18) | copy-start | bytes 3145732
  628.0 5.5 copy-start.4
  645.8 4.3 copy-start.15
  (17 other events, 41.6 us)
Sparse Core Ops, SparseCore 0:
  117.7 76.7 all-reduce.6
  203.7 75.7 reduce-scatter.9
  282.8 75.0 reduce-scatter.11
  361.7 75.0 reduce-scatter.13
  444.3 169.6 all-reduce.4
